TPU v7x, 768 devices: a whole 4x8x12 slice. The times are simulated.
768 devices in a mesh: lon: 192 (over x, y_hi, z, core), lat: 4 (over y_lo).
Axes of the slice: x: 4, y: 8 (y_hi: 2, y_lo: 4; y = y_hi * 4 + y_lo), z: 12, core: 2. Of those that a mesh axis runs over, the one named last changes fastest.
Arguments:
- thermal_anomaly: float32 [75, 384, 512], P(None, 'lon', 'lat'), may hold values from -6 to 6
- saltiness_anomaly: float32 [75, 384, 512], P(None, 'lon', 'lat'), may hold values from -6 to 6
- zonal_flow: float32 [75, 384, 512], P(None, 'lon', 'lat'), may hold values from -3 to 3
- meridional_flow: float32 [75, 384, 512], P(None, 'lon', 'lat'), may hold values from -3 to 3
- flooded_layer_number: int32 [384, 512], P('lon', 'lat'), may hold values from 0 to 75
- sideways_diffusion: float32 [384, 512], P('lon', 'lat'), may hold values from 0.2 to 4
- ambient_diffusion: float32 [384, 512], P('lon', 'lat'), may hold values from 0.1 to 10
Outputs:
- temp_next: float32 [75, 384, 512], P(None, 'lon', 'lat')
- salt_next: float32 [75, 384, 512], P(None, 'lon', 'lat')
- u_next: float32 [75, 384, 512], P(None, 'lon', 'lat')
- v_next: float32 [75, 384, 512], P(None, 'lon', 'lat')
Inputs may be any that keep to these rules, and one draw needn't show every extreme that they name: flooded_layer_number counts wet levels from the top; 0 marks land.
All inputs are finite; a program needn't handle non-finite values.
Results may differ from a plain program's by a relative error of at most 0.0003.
Values sent between devices are 32-bit elements; how exact they have to be, the bound alone decides.
A program may use at most 64 MiB of HBM per device.

v0:
```python
import jax
import jax.numpy as jnp
from jax import lax
from jax.sharding import Mesh
from jax.sharding import PartitionSpec as P

SUBSTEPS = 2
LON = ("lon_0", "lon_1", "lon_2", "lon_3")


dt_step = 0.05


def extended(x, sides, width):
    for axis, dim in sides:
        devices, length = (lax.axis_size(axis), x.shape[dim])
        up = [(i, (i + 1) % devices) for i in range(devices)]
        down = [(j, i) for i, j in up]
        last = lax.slice_in_dim(x, length - width, length, axis=dim)
        first = lax.slice_in_dim(x, 0, width, axis=dim)
        before = lax.ppermute(last, axis, up)
        after = lax.ppermute(first, axis, down)
        x = jnp.concatenate([before, x, after], axis=dim)
    return x


def joined_along(tiles, dim):
    tiles = jnp.moveaxis(tiles, 0, dim)
    shape = tiles.shape
    return tiles.reshape(*shape[:dim], shape[dim] * shape[dim + 1], *shape[dim + 2 :])


def all_blocks(x, axes, order):
    tiles = x[None]
    for k in order:
        tiles = lax.all_gather(tiles, axes[k], axis=0, tiled=True)
    current = [lax.axis_size(axes[k]) for k in reversed(order)]
    tiles = tiles.reshape(*current, *x.shape)
    turned = sorted(range(len(order)), key=lambda place: order[len(order) - 1 - place])
    return tiles.transpose(*turned, *range(len(order), tiles.ndim)).reshape(-1, *x.shape)


def gather_axes(x, axes, order, dim):
    return joined_along(all_blocks(x, axes, order), dim)


def density(temp_field, salt_field):
    return (
        0.8 * salt_field
        - 0.2 * temp_field
        - 0.05 * temp_field * temp_field
        + 0.03 * temp_field * salt_field
    )


def coriolis_rows(first_row, row_total, total_rows):
    row_index = first_row + jnp.arange(row_total, dtype=jnp.int32)
    mirrored = jnp.where(row_index >= total_rows, 2 * total_rows - 1 - row_index, row_index)
    return 0.2 + mirrored.astype(jnp.float32) / total_rows


def centre(array):
    return array[..., 1:-1, 1:-1]


def to_east(array):
    return array[..., 2:, 1:-1]


def to_west(array):
    return array[..., :-2, 1:-1]


def to_north(array):
    return array[..., 1:-1, 2:]


def to_south(array):
    return array[..., 1:-1, :-2]


def advance(padded, planet):
    layer_total = (padded.shape[0] - 2) // 4
    marine_state = padded[: 4 * layer_total].reshape(
        4, layer_total, padded.shape[1], padded.shape[2]
    )
    bottom = padded[4 * layer_total]
    lateral = padded[4 * layer_total + 1]
    level_index = jnp.arange(layer_total, dtype=jnp.float32)[:, None, None]
    wet_mask = (level_index < bottom[None]).astype(jnp.float32)
    pressure = 0.5 * jnp.cumsum(density(marine_state[0], marine_state[1]), axis=0)
    wet_centre = centre(wet_mask)
    lateral_centre = centre(lateral)
    field_centre = centre(marine_state)
    lateral_mix = jnp.zeros_like(field_centre)
    for neighbour in (to_east, to_west, to_north, to_south):
        face_coef = 0.5 * (lateral_centre + neighbour(lateral)) * wet_centre * neighbour(wet_mask)
        lateral_mix = lateral_mix + face_coef * (neighbour(marine_state) - field_centre)
    u_centre = field_centre[2]
    v_centre = field_centre[3]
    advection = (
        u_centre * (to_east(marine_state) - to_west(marine_state)) * 0.5
        + v_centre * (to_north(marine_state) - to_south(marine_state)) * 0.5
    )
    tendency = lateral_mix - advection
    planet_rows = planet[1:-1]
    tend_u = tendency[2] + planet_rows * v_centre - (to_east(pressure) - to_west(pressure)) * 0.5
    tend_v = tendency[3] - planet_rows * u_centre - (to_north(pressure) - to_south(pressure)) * 0.5
    tendency = jnp.stack([tendency[0], tendency[1], tend_u, tend_v])
    updated = wet_centre * (field_centre + dt_step * tendency)
    return updated.reshape(4 * layer_total, updated.shape[2], updated.shape[3])


def vertical_mix(marine_state, wet_mask, ambient_diffusion):
    layer_total = marine_state.shape[1]
    density_now = density(marine_state[0], marine_state[1])
    stratification = density_now[1:] - density_now[:-1]
    coupling = (
        ambient_diffusion[None]
        * (0.2 + 1.0 / (1.0 + 10.0 * jnp.maximum(stratification, 0.0)))
        * wet_mask[1:]
    )
    zero_plane = jnp.zeros_like(ambient_diffusion)
    ratio_prev = zero_plane
    value_prev = jnp.zeros_like(marine_state[:, 0])
    ratio_list = []
    value_list = []
    for level in range(layer_total):
        lower_coef = coupling[level - 1] if level > 0 else zero_plane
        upper_coef = coupling[level] if level < layer_total - 1 else zero_plane
        pivot_value = 1.0 + lower_coef + upper_coef + lower_coef * ratio_prev
        ratio_prev = -upper_coef / pivot_value
        value_prev = (marine_state[:, level] + lower_coef * value_prev) / pivot_value
        ratio_list.append(ratio_prev)
        value_list.append(value_prev)
    current = value_list[layer_total - 1]
    solved = [current]
    for level in range(layer_total - 2, -1, -1):
        current = value_list[level] - ratio_list[level] * current
        solved.append(current)
    return jnp.stack(solved[::-1], axis=1)


def extend(state_stack, fold_signs, margin):
    lon_index = lax.axis_index(LON)
    lat_index = lax.axis_index("lat")
    lon_count = lax.axis_size(LON)
    lat_count = lax.axis_size("lat")
    column_count = state_stack.shape[1]
    meridian_total = state_stack.shape[2]
    pivot_offset = column_count // 2
    padded = extended(state_stack, ((LON, 1), ("lat", 2)), margin)
    top_rows = state_stack[:, :, meridian_total - margin :][:, :, ::-1]
    total_cols = column_count * lon_count
    positions = (
        lon_index * column_count - margin + jnp.arange(column_count + 2 * margin, dtype=jnp.int32)
    )
    source = jnp.mod(total_cols - 1 - pivot_offset - positions, total_cols)
    every_top = gather_axes(top_rows, LON, (1, 0, 2, 3), 1)
    folded = jnp.take(every_top, source, axis=1)
    folded = folded * fold_signs[:, None, None]
    padded_rows = padded.shape[2]
    edge_low = jnp.where(lat_index > 0, padded[:, :, :margin], 0.0)
    edge_high = jnp.where(lat_index == lat_count - 1, folded, padded[:, :, padded_rows - margin :])
    return jnp.concatenate(
        [edge_low, padded[:, :, margin : padded_rows - margin], edge_high], axis=2
    )


def shards(
    thermal_anomaly,
    saltiness_anomaly,
    zonal_flow,
    meridional_flow,
    flooded_layer_number,
    sideways_diffusion,
    ambient_diffusion,
):
    layer_total = thermal_anomaly.shape[0]
    meridian_total = thermal_anomaly.shape[2]
    lat_index = lax.axis_index("lat")
    total_rows = meridian_total * lax.axis_size("lat")
    statics = jnp.stack([flooded_layer_number.astype(jnp.float32), sideways_diffusion])
    marine_state = jnp.concatenate(
        [thermal_anomaly, saltiness_anomaly, zonal_flow, meridional_flow], axis=0
    )
    fold_signs = jnp.concatenate(
        [
            jnp.ones((2 * layer_total,), jnp.float32),
            -jnp.ones((2 * layer_total,), jnp.float32),
            jnp.ones((2,), jnp.float32),
        ]
    )
    padded = extend(jnp.concatenate([marine_state, statics], axis=0), fold_signs, SUBSTEPS)
    for substep in range(SUBSTEPS):
        margin = SUBSTEPS - substep
        planet = coriolis_rows(
            lat_index * meridian_total - margin, meridian_total + 2 * margin, total_rows
        )
        marine_state = advance(padded, planet)
        padded = jnp.concatenate([marine_state, padded[4 * layer_total :, 1:-1, 1:-1]], axis=0)
    level_index = jnp.arange(layer_total, dtype=jnp.float32)[:, None, None]
    wet_mask = (level_index < flooded_layer_number.astype(jnp.float32)[None]).astype(jnp.float32)
    final = vertical_mix(
        marine_state.reshape(4, layer_total, marine_state.shape[1], marine_state.shape[2]),
        wet_mask,
        ambient_diffusion,
    )
    return (final[0], final[1], final[2], final[3])


def solution(mesh):
    split = Mesh(
        mesh.devices.reshape(4, 2, 12, 2, mesh.shape["lat"]),
        ("lon_0", "lon_1", "lon_2", "lon_3", "lat"),
    )
    return jax.shard_map(
        shards,
        mesh=split,
        in_specs=(
            P(None, LON, "lat"),
            P(None, LON, "lat"),
            P(None, LON, "lat"),
            P(None, LON, "lat"),
            P(LON, "lat"),
            P(LON, "lat"),
            P(LON, "lat"),
        ),
        out_specs=(
            P(None, LON, "lat"),
            P(None, LON, "lat"),
            P(None, LON, "lat"),
            P(None, LON, "lat"),
        ),
        check_vma=False,
    )
```

profile of v0, /device:TPU:56, one launch (start us, length us, event | category | flops | bytes accessed | tf_op | source)
XLA Modules:
  0.0 126.5 jit_solution(1882662966096892425)
XLA Ops:
  0.6 0.7 fusion.178
  1.3 0.1 copy.766
  1.5 1.0 copy.762
  2.4 1.0 copy.763
  3.4 1.0 copy.764
  4.4 1.0 copy.765
  5.4 0.8 copy.767
  6.2 0.3 concatenate.9
  6.5 16.3 %collective-permute-start.1 = (f32[302,2,128]{0,2,1:T(8,128)S(1)}, f32[302,2,128]{0,2,1:T(8,128)S(1)}, u32[]{:S(2)}, u32[]{:S(2)}) collective-permute-start(f32[302,2,128]{0,2,1:T(8,128)S(1)} %concatenate.9), channel_id=1, source_target_pairs={{4,0},{8,4},{12,8},{16,12},{20,16},{24,20},{28,24},{32,28},{36,32}... | collective-permute-start | bytes 927752 | tf_op jit(solution)/shard_map/ppermute | solution.py:22
  22.8 1.9 %collective-permute-start = (f32[302,2,128]{0,2,1:T(8,128)S(1)}, f32[302,2,128]{0,2,1:T(8,128)S(1)}, u32[]{:S(2)}, u32[]{:S(2)}) collective-permute-start(f32[302,2,128]{0,2,1:T(8,128)S(1)} %concatenate.9), channel_id=1, source_target_pairs={{0,4},{4,8},{8,12},{12,16},{16,20},{20,24},{24,28},{28,32},{32,36}... | collective-permute-start | bytes 927752 | tf_op jit(solution)/shard_map/ppermute | solution.py:21
  24.9 0.2 copy.768
  25.2 24.4 %all-gather = f32[604,2,2]{2,1,0:T(2,128)S(1)} all-gather(f32[302,2,2]{2,1,0:T(2,128)S(1)} %copy.768), channel_id=2, replica_groups=mesh['lon_0'=4,'lon_1'=2,'lon_2'=12,'lon_3'=2,'lat'=4] {'lon_1'}, dimensions={0}, use_global_device_ids=true | all-gather | bytes 14496 | tf_op jit(solution)/shard_map/all_gather | solution.py:36
  49.6 0.3 copy.769
  49.9 11.9 %all_gather.13 = f32[8,302,2,2]{1,3,2,0:T(2,128)S(1)} all-gather(f32[2,302,2,2]{1,3,2,0:T(2,128)S(1)} %copy.769), channel_id=1, replica_groups=mesh['lon_0'=4,'lon_1'=2,'lon_2'=12,'lon_3'=2,'lat'=4] {'lon_0'}, dimensions={0}, use_global_device_ids=true | all-gather | bytes 48320 | tf_op jit(solution)/shard_map/all_gather | solution.py:36
  61.8 26.8 %all_gather.14 = f32[96,302,2,2]{1,3,2,0:T(2,128)S(1)} all-gather(f32[8,302,2,2]{1,3,2,0:T(2,128)S(1)} %all_gather.13), channel_id=1, replica_groups=mesh['lon_0'=4,'lon_1'=2,'lon_2'=12,'lon_3'=2,'lat'=4] {'lon_2'}, dimensions={0}, use_global_device_ids=true | all-gather | bytes 502528 | tf_op jit(solution)/shard_map/all_gather | solution.py:36
  88.6 2.6 %all_gather.15 = f32[192,302,2,2]{1,3,2,0:T(2,128)S(1)} all-gather(f32[96,302,2,2]{1,3,2,0:T(2,128)S(1)} %all_gather.14), channel_id=1, replica_groups=mesh['lon_0'=4,'lon_1'=2,'lon_2'=12,'lon_3'=2,'lat'=4] {'lon_3'}, dimensions={0}, use_global_device_ids=true | all-gather | bytes 1391616 | tf_op jit(solution)/shard_map/all_gather | solution.py:36
  91.3 4.5 %collective-permute-start.2 = (f32[302,6,2]{0,2,1:T(2,128)S(1)}, f32[302,6,2]{0,2,1:T(2,128)S(1)}, u32[]{:S(2)}, u32[]{:S(2)}) collective-permute-start(f32[302,6,2]{0,2,1:T(2,128)S(1)} %get-tuple-element.257), channel_id=1, source_target_pairs={{0,1},{1,2},{2,3},{3,0},{4,5},{5,6},{6,7},{7,4},{8,9},{9,10},{10,1... | collective-permute-start | bytes 43496 | tf_op jit(solution)/shard_map/ppermute | solution.py:21
  96.0 0.4 copy.770
  96.4 0.6 gather_fusion
  97.0 1.9 %collective-permute-start.3 = (f32[302,6,2]{0,2,1:T(2,128)S(1)}, f32[302,6,2]{0,2,1:T(2,128)S(1)}, u32[]{:S(2)}, u32[]{:S(2)}) collective-permute-start(f32[302,6,2]{0,2,1:T(2,128)S(1)} %get-tuple-element.258), channel_id=1, source_target_pairs={{1,0},{2,1},{3,2},{0,3},{5,4},{6,5},{7,6},{4,7},{9,8},{10,9},{11,1... | collective-permute-start | bytes 43496 | tf_op jit(solution)/shard_map/ppermute | solution.py:22
  99.0 5.5 %collective-permute-done.3 = f32[302,6,2]{0,2,1:T(2,128)S(1)} collective-permute-done((f32[302,6,2]{0,2,1:T(2,128)S(1)}, f32[302,6,2]{0,2,1:T(2,128)S(1)}, u32[]{:S(2)}, u32[]{:S(2)}) %collective-permute-start.3) | collective-permute-done | bytes 14528 | tf_op jit(solution)/shard_map/ppermute | solution.py:22
  104.6 0.1 pad_maximum_fusion
  104.7 0.6 slice_reduce_fusion.2
  105.3 0.8 slice_reduce_fusion
  106.1 0.2 fusion.4
  106.3 0.4 copy.772
  106.8 0.9 broadcast_multiply_fusion
  107.7 3.1 %copy.771 = f32[300,6,132]{2,1,0:T(8,128)S(1)} copy(f32[300,6,132]{0,2,1:T(8,128)} %bitcast.1380) | data formatting | bytes 1900800 | tf_op jit(solution)/shard_map/slice | solution.py:84
  110.8 0.4 slice_bitcast_fusion.5
  111.2 0.7 fusion.173
  111.9 2.8 %multiply_subtract_fusion = f32[4,75,4,130]{3,2,1,0:T(4,128)S(1)} fusion(f32[4,75,6,132]{3,2,1,0:T(8,128)S(1)} %bitcast.1377, f32[75,4,130]{2,1,0:T(4,128)S(1)} %get-tuple-element.248, f32[75,4,130]{2,1,0:T(4,128)S(1)} %get-tuple-element.247, f32[75,4,130]{2,1,0:T(4,128)S(1)} %get-tuple-element.260, f32[75,4,130]{2,1,0:T(4,128)S(1)} %get-tuple-element.261, ...), kind=kLoop, calls=%fused_computation.5 | loop fusion | flops 2808000 | bytes 4680000 | tf_op jit(solution)/shard_map/sub | solution.py:105
  114.9 0.9 copy-done.1
  115.9 0.9 fusion.15
  116.7 0.8 fusion.1
  117.6 0.2 slice_bitcast_fusion.9
  117.8 0.2 broadcast_multiply_fusion.1
  118.2 0.4 fusion.176
  118.6 1.3 %fusion.172 = (f32[4,75,2,128]{3,2,1,0:T(2,128)S(1)}, f32[4,75,2,128]{3,2,1,0:T(2,128)S(1)}, f32[4,75,2,128]{3,2,1,0:T(2,128)S(1)}, f32[4,75,2,128]{3,2,1,0:T(2,128)S(1)}) fusion(f32[4,75,4,130]{3,2,1,0:T(4,128)S(1)} %fusion.1, f32[75,2,128]{2,1,0:T(2,128)S(1)} %get-tuple-element.272, f32[75,2,128]{2,1,0:T(2,128)S(1)} %get-tuple-element.273, ...), kind=kLoop, calls=%fused_computation.673 | loop fusion | flops 1075200 | bytes 3148800 | tf_op jit(solution)/shard_map/slice | solution.py:63
  120.0 0.3 copy_subtract_fusion
  120.4 0.1 fusion.177
  120.5 0.5 fusion.35
  121.0 0.3 fusion.18
  121.7 0.7 multiply_add_fusion.1
  122.4 0.4 fusion.127
  122.8 0.2 fusion.76
  123.0 0.4 constant_dynamic-update-slice_fusion.74
  123.6 1.2 constant_dynamic-update-slice_fusion.62
  125.6 0.9 fusion.174
  (112 shorter events, 2.0 us)
Async XLA Ops:
  6.5 84.7 %collective-permute-start.1 = (f32[302,2,128]{0,2,1:T(8,128)S(1)}, f32[302,2,128]{0,2,1:T(8,128)S(1)}, u32[]{:S(2)}, u32[]{:S(2)}) collective-permute-start(f32[302,2,128]{0,2,1:T(8,128)S(1)} %concatenate.9), channel_id=1, source_target_pairs={{4,0},{8,4},{12,8},{16,12},{20,16},{24,20},{28,24},{32,28},{36,32}... | collective-permute-start | bytes 927752 | tf_op jit(solution)/shard_map/ppermute | solution.py:22
  22.8 68.5 %collective-permute-start = (f32[302,2,128]{0,2,1:T(8,128)S(1)}, f32[302,2,128]{0,2,1:T(8,128)S(1)}, u32[]{:S(2)}, u32[]{:S(2)}) collective-permute-start(f32[302,2,128]{0,2,1:T(8,128)S(1)} %concatenate.9), channel_id=1, source_target_pairs={{0,4},{4,8},{8,12},{12,16},{16,20},{20,24},{24,28},{28,32},{32,36}... | collective-permute-start | bytes 927752 | tf_op jit(solution)/shard_map/ppermute | solution.py:21
  91.3 4.7 %copy-start.2 = (f32[302,2,128]{0,2,1:T(8,128)}, f32[302,2,128]{0,2,1:T(8,128)S(1)}, u32[]{:S(2)}) copy-start(f32[302,2,128]{0,2,1:T(8,128)S(1)} %collective-permute-done) | copy-start | bytes 927748
  91.3 7.7 %collective-permute-start.2 = (f32[302,6,2]{0,2,1:T(2,128)S(1)}, f32[302,6,2]{0,2,1:T(2,128)S(1)}, u32[]{:S(2)}, u32[]{:S(2)}) collective-permute-start(f32[302,6,2]{0,2,1:T(2,128)S(1)} %get-tuple-element.257), channel_id=1, source_target_pairs={{0,1},{1,2},{2,3},{3,0},{4,5},{5,6},{6,7},{7,4},{8,9},{9,10},{10,1... | collective-permute-start | bytes 43496 | tf_op jit(solution)/shard_map/ppermute | solution.py:21
  96.4 8.1 %copy-start.4 = (f32[302]{0:T(512)S(1)}, f32[302]{0:T(512)}, u32[]{:S(2)}) copy-start(f32[302]{0:T(512)} %constant.47.clone.1) | copy-start | bytes 3628
  96.4 8.1 %copy-start.3 = (f32[302,2,128]{0,2,1:T(8,128)S(1)}, f32[302,2,128]{0,2,1:T(8,128)}, u32[]{:S(2)}) copy-start(f32[302,2,128]{0,2,1:T(8,128)} %copy-done.2) | copy-start | bytes 927748
  97.0 7.5 %collective-permute-start.3 = (f32[302,6,2]{0,2,1:T(2,128)S(1)}, f32[302,6,2]{0,2,1:T(2,128)S(1)}, u32[]{:S(2)}, u32[]{:S(2)}) collective-permute-start(f32[302,6,2]{0,2,1:T(2,128)S(1)} %get-tuple-element.258), channel_id=1, source_target_pairs={{1,0},{2,1},{3,2},{0,3},{5,4},{6,5},{7,6},{4,7},{9,8},{10,9},{11,1... | collective-permute-start | bytes 43496 | tf_op jit(solution)/shard_map/ppermute | solution.py:22
  104.7 1.5 %copy-start = (f32[302,6,132]{0,2,1:T(8,128)}, f32[302,6,132]{0,2,1:T(8,128)S(1)}, u32[]{:S(2)}) copy-start(f32[302,6,132]{0,2,1:T(8,128)S(1)} %pad_maximum_fusion) | copy-start | bytes 2870212
  114.8 1.1 copy-start.1
  120.5 1.0 copy-start.5
where the time goes:
time: 127 us
  blocking collectives  65.8 us (52%)
  starting transfers between devices  24.6 us (19%)
  local copies, waits for them, and re-layouts  15.1 us (12%)
  other arithmetic  14.3 us (11%)
  waiting for transfers between devices  5.5 us (4%)
  between operations  1.28 us (1%)
    all_gather x4, blocking collectives, all_blocks(): tiles = lax.all_gather(tiles, axes[k], axis=0, tiled=True)  65.8 us
    ppermute x2, starting transfers between devices, extended(): after = lax.ppermute(first, axis, down)  18.2 us
    ppermute x2, starting transfers between devices, extended(): before = lax.ppermute(last, axis, up)  6.44 us
    ppermute x2, waiting for transfers between devices, extended(): after = lax.ppermute(first, axis, down)  5.5 us
    unnamed x52, local copies, waits for them, and re-layouts  5.25 us
    sub x2, other arithmetic, advance(): tendency = lateral_mix - advection  3.19 us
    slice x1, local copies, waits for them, and re-layouts, advance(): padded[:4 * layer_total]  3.09 us
  transfers between devices with their start and end apart: 4, of which 1 were waited for; matrix products, arithmetic and copies ran while one was open for 1% of the time, Pallas kernels for 0%

commit v1 on v0

v1 whole, which is shorter than its diff:
```python
import functools

import jax
import jax.numpy as jnp
from jax import lax
from jax.experimental import pallas as pl
from jax.experimental.pallas import tpu as pltpu
from jax.sharding import PartitionSpec as P

MESH = pl.DeviceIdType.MESH
DT = 0.05
FIELDS = 4
COLUMNS = 2
SPAN = 128
LEVELS = 4
ROWS = LEVELS * COLUMNS
CHUNK = 4


def density(t, s):
    return s * (0.8 + 0.03 * t) - t * (0.2 + 0.05 * t)


def up(x, n):
    return pltpu.roll(x, n % ROWS, 0)


def along(x, n):
    return pltpu.roll(x, n % SPAN, 1)


def halo_and_levels(
    levels, lon_count, lat_count,
    t_in, s_in, u_in, v_in, flooded_in, lateral_in, ambient_in,
    y_out, r_out,
    own, east_tile, west_tile, flooded, lateral, ambient, pack, halo_n, halo_s, rim, rim_x, rim_new,
    local_sem, ew_send, ew_recv, static_send, static_recv, edge_send, edge_recv,
):
    fields_in = (t_in, s_in, u_in, v_in)
    groups = pl.cdiv(levels, LEVELS)
    me = lax.axis_index("lon")
    row = lax.axis_index("lat")
    east = lax.rem(me + 1, lon_count)
    west = lax.rem(me + lon_count - 1, lon_count)
    fold_a = lon_count - 1 - me
    fold_b = lax.rem(2 * lon_count - 2 - me, lon_count)
    top = row == lat_count - 1
    bottom = row == 0
    inner = jnp.logical_not(top)
    above = jnp.logical_not(bottom)
    b_other = jnp.logical_and(top, fold_b != me)
    b_self = jnp.logical_and(top, fold_b == me)
    north = row + 1
    south = row - 1

    barrier = pltpu.get_barrier_semaphore()

    def greet(lon, lat):
        pl.semaphore_signal(barrier, inc=1, device_id=(lon, lat), device_id_type=MESH)

    greet(east, row)
    greet(west, row)

    @pl.when(top)
    def _():
        greet(fold_a, row)

    @pl.when(b_other)
    def _():
        greet(fold_b, row)

    @pl.when(inner)
    def _():
        greet(me, north)
        greet(east, north)
        greet(west, north)

    @pl.when(above)
    def _():
        greet(me, south)
        greet(east, south)
        greet(west, south)

    flat = [x.reshape(levels * COLUMNS, SPAN) for x in fields_in]
    local = [
        pltpu.make_async_copy(flat[f], own.at[f, 0:levels * COLUMNS], local_sem.at[f])
        for f in range(FIELDS)
    ]
    local += [
        pltpu.make_async_copy(flooded_in, flooded.at[0], local_sem.at[4]),
        pltpu.make_async_copy(lateral_in, lateral.at[0], local_sem.at[5]),
        pltpu.make_async_copy(ambient_in, ambient, local_sem.at[6]),
    ]
    for copy in local:
        copy.start()
    for copy in local:
        copy.wait()

    lane = lax.broadcasted_iota(jnp.int32, (ROWS, SPAN), 1)
    sub = lax.broadcasted_iota(jnp.int32, (ROWS, SPAN), 0)
    quad = lane // 4
    place = lane % 4
    tier = sub // COLUMNS
    even = sub % COLUMNS == 0

    def tiled(x):
        return jnp.concatenate([x.astype(jnp.float32)] * LEVELS, axis=0)

    depth_own = tiled(flooded[0])
    mix_own = tiled(lateral[0])
    for f in range(FIELDS):
        def edges(g, acc):
            at = pl.multiple_of(g * ROWS, ROWS)
            return jnp.where(quad == g, pltpu.roll(own[f, pl.ds(at, ROWS)], 4 * g + 2, 1), acc)

        acc = lax.fori_loop(0, groups, edges, jnp.zeros((ROWS, SPAN), jnp.float32), unroll=True)
        if f == 0:
            acc = jnp.where(quad == groups, along(depth_own, 4 * groups + 2), acc)
            acc = jnp.where(quad == groups + 1, along(mix_own, 4 * groups + 6), acc)
        pack[f] = acc

    waits = (
        2 + 3 * inner.astype(jnp.int32) + 3 * above.astype(jnp.int32)
        + top.astype(jnp.int32) + b_other.astype(jnp.int32)
    )
    pl.semaphore_wait(barrier, waits)

    def edge(slot, lon, lat, sent):
        dst = halo_s if slot < 3 else halo_n
        return pltpu.make_async_remote_copy(
            src_ref=pack, dst_ref=dst.at[slot % 3],
            send_sem=edge_send.at[sent], recv_sem=edge_recv.at[slot],
            device_id=(lon, lat), device_id_type=MESH,
        )

    to_a = edge(3, fold_a, row, 6)
    to_b = edge(4, fold_b, row, 7)
    b_copy = pltpu.make_async_copy(pack, halo_n.at[1], local_sem.at[7])
    northward = (edge(0, me, north, 0), edge(1, west, north, 1), edge(2, east, north, 2))
    southward = (edge(3, me, south, 3), edge(4, west, south, 4), edge(5, east, south, 5))

    @pl.when(top)
    def _():
        to_a.start()

    @pl.when(b_other)
    def _():
        to_b.start()

    @pl.when(b_self)
    def _():
        b_copy.start()

    @pl.when(inner)
    def _():
        for copy in northward:
            copy.start()

    @pl.when(above)
    def _():
        for copy in southward:
            copy.start()

    sides = ((east, west_tile), (west, east_tile))
    statics = []
    for side, (lon, _) in enumerate(sides):
        for n, (src, dst) in enumerate(((flooded_in, flooded), (lateral_in, lateral))):
            statics.append(pltpu.make_async_remote_copy(
                src_ref=src, dst_ref=dst.at[1 + side],
                send_sem=static_send.at[side, n], recv_sem=static_recv.at[side, n],
                device_id=(lon, row), device_id_type=MESH,
            ))
    starts = list(range(0, groups, CHUNK))
    tiles = []
    for c, first in enumerate(starts):
        lo = first * ROWS
        hi = min((first + CHUNK) * ROWS, levels * COLUMNS)
        part = []
        for f in range(FIELDS):
            for side, (lon, dst) in enumerate(sides):
                part.append(pltpu.make_async_remote_copy(
                    src_ref=flat[f].at[lo:hi], dst_ref=dst.at[f, lo:hi],
                    send_sem=ew_send.at[side, c, f], recv_sem=ew_recv.at[side, c, f],
                    device_id=(lon, row), device_id_type=MESH,
                ))
        tiles.append(part)
    for copy in statics:
        copy.start()
    for part in tiles:
        for copy in part:
            copy.start()

    for copy in statics:
        copy.wait_recv()

    @pl.when(above)
    def _():
        for copy in northward:
            copy.wait_recv()

    @pl.when(inner)
    def _():
        for copy in southward:
            copy.wait_recv()

    @pl.when(top)
    def _():
        to_a.wait_recv()

    @pl.when(b_other)
    def _():
        to_b.wait_recv()

    @pl.when(b_self)
    def _():
        b_copy.wait()

    def sideways(o, x):
        return jnp.where(even, up(o, -1), up(x, 1)), jnp.where(even, up(x, -1), up(o, 1))

    def prefix(d):
        two = up(d, COLUMNS)
        s = d + jnp.where(tier >= 1, two, 0.0)
        pair = d + two
        return s + jnp.where(tier >= 2, up(s, 2 * COLUMNS), 0.0), pair + up(pair, 2 * COLUMNS)

    def packed_pressure(t, s):
        inside, total = prefix(0.5 * density(t, s))
        for n in (4, 8, 16, 32, 64):
            total = total + jnp.where(lane >= n, along(total, n), 0.0)
        return inside + jnp.where(lane >= 4, along(total, 4), 0.0)

    def every_quad(x, n):
        x = jnp.where(quad == n, x, 0.0)
        for n in (4, 8, 16, 32, 64):
            x = x + along(x, n)
        return x

    for f in range(FIELDS):
        sign = 1.0 if f < 2 else -1.0
        n0, n1, n2 = halo_n[0, f], halo_n[1, f], halo_n[2, f]
        s0, s1, s2 = halo_s[0, f], halo_s[1, f], halo_s[2, f]
        for dst, n, s, fold in (
            (rim, n0, s0, jnp.where(even, n0, n1)),
            (rim_x, jnp.where(even, n1, n2), jnp.where(even, s1, s2), jnp.where(even, n1, n0)),
        ):
            n = jnp.where(place == 1, along(n, -1), along(n, -3))
            n = jnp.where(top, sign * fold, n)
            s = jnp.where(place == 2, along(s, 1), along(s, 3))
            s = jnp.where(bottom, 0.0, s)
            dst[f] = jnp.where(place < 2, n, s)

    def turning(j):
        total = lat_count * SPAN
        m = jnp.where(j >= total, 2 * total - 1 - j, j)
        return DT * (0.2 + m.astype(jnp.float32) / total)

    def faces(depth, mix, sides_of):
        return [(jnp.minimum(depth, d), mix + m) for d, m in zip(sides_of(0), sides_of(1))]

    def weights(level, depth, around):
        c = [jnp.where(level < d, m, 0.0) for d, m in around]
        return c, 1.0 - ((c[0] + c[1]) + (c[2] + c[3])), level < depth

    def update(weight, turn, cells, e, w, n, s):
        (ce, cw, cn, cs), keep, wet = weight
        half_u = (0.5 * DT) * cells[2]
        half_v = (0.5 * DT) * cells[3]
        ce, cw, cn, cs = ce - half_u, cw + half_u, cn - half_v, cs + half_v
        out = []
        for f in range(FIELDS):
            x = (keep * cells[f] + ce * e[f]) + (cw * w[f] + (cn * n[f] + cs * s[f]))
            if f == 2:
                x = x + (turn * cells[3] - (0.5 * DT) * (e[4] - w[4]))
            if f == 3:
                x = x - (turn * cells[2] + (0.5 * DT) * (n[4] - s[4]))
            out.append(jnp.where(wet, x, 0.0))
        return out

    own_edge = [pack[f] for f in range(FIELDS)]
    cells = [rim[f] for f in range(FIELDS)]
    cells_x = [rim_x[f] for f in range(FIELDS)]
    rim_depth, rim_mix = every_quad(cells[0], groups), (0.5 * DT) * every_quad(cells[0], groups + 1)
    x_depth, x_mix = every_quad(cells_x[0], groups), (0.5 * DT) * every_quad(cells_x[0], groups + 1)
    o_depth, o_mix = every_quad(own_edge[0], groups), (0.5 * DT) * every_quad(own_edge[0], groups + 1)
    for block in (own_edge, cells, cells_x):
        block.append(packed_pressure(block[0], block[1]))
    rim[4] = cells[4]
    rim_x[4] = cells_x[4]

    def around_rim(c, x, o):
        e, w = sideways(c, x)
        return e, w, jnp.where(place == 1, along(c, 1), o), jnp.where(place == 2, along(c, -1), o)

    around = [around_rim(*q) for q in zip(cells, cells_x, own_edge)]
    statics_around = (around_rim(rim_depth, x_depth, o_depth), around_rim(rim_mix, x_mix, o_mix))
    rim_level = (LEVELS * quad + tier).astype(jnp.float32)
    rim_row = jnp.where(place < 2, (row + 1) * SPAN + 1 - place, row * SPAN + 1 - place)
    new = update(
        weights(rim_level, rim_depth, faces(rim_depth, rim_mix, lambda n: statics_around[n])),
        turning(rim_row), cells, *[[q[n] for q in around] for n in range(4)],
    )
    new.append(packed_pressure(new[0], new[1]))
    for q in range(FIELDS + 1):
        rim_new[q] = new[q]

    first_lane = lane == 0
    last_lane = lane == SPAN - 1

    def beside(x, r):
        return jnp.where(last_lane, r, along(x, -1)), jnp.where(first_lane, r, along(x, 1))

    def shifted(x, g):
        return pltpu.roll(x, lax.rem(2 * SPAN - 2 - 4 * g, SPAN) if not isinstance(g, int) else (-2 - 4 * g) % SPAN, 1)

    def around_own(o, x, r):
        return sideways(o, x) + beside(o, r)

    def around_x(o, x, z, r):
        return (jnp.where(even, z, up(o, 1)), jnp.where(even, up(o, -1), z)) + beside(x, r)

    def split(e, w):
        return jnp.where(even, e, w), jnp.where(even, up(e, -1), up(w, 1))

    depth_x, depth_z = split(tiled(flooded[2]), tiled(flooded[1]))
    mix_x, mix_z = split(tiled(lateral[2]), tiled(lateral[1]))
    mix_o, mix_x, mix_z = ((0.5 * DT) * x for x in (mix_own, mix_x, mix_z))
    rim_depth_at, rim_mix_at = shifted(rim_depth, 0), shifted(rim_mix, 0)
    x_depth_at, x_mix_at = shifted(x_depth, 0), shifted(x_mix, 0)
    own_statics = (around_own(depth_own, depth_x, rim_depth_at), around_own(mix_o, mix_x, rim_mix_at))
    x_statics = (
        around_x(depth_own, depth_x, depth_z, x_depth_at), around_x(mix_o, mix_x, mix_z, x_mix_at)
    )
    own_faces = faces(depth_own, mix_o, lambda n: own_statics[n])
    x_faces = faces(depth_x, mix_x, lambda n: x_statics[n])
    turn = turning(row * SPAN + lane)
    ambient_all = tiled(ambient[...])
    tier_level = tier.astype(jnp.float32)
    low = tier % 2 == 0
    lower_half = tier < 2

    def per_level(blocks):
        a, b, c, d = blocks
        ab0, ab1 = jnp.where(low, a, up(b, 2)), jnp.where(low, up(a, -2), b)
        cd0, cd1 = jnp.where(low, c, up(d, 2)), jnp.where(low, up(c, -2), d)
        return (
            jnp.where(lower_half, ab0, up(cd0, 4)), jnp.where(lower_half, ab1, up(cd1, 4)),
            jnp.where(lower_half, up(ab0, 4), cd0), jnp.where(lower_half, up(ab1, 4), cd1),
        )

    def repeated(a):
        ab0, ab1 = jnp.where(low, a, up(a, 2)), jnp.where(low, up(a, -2), a)
        r0, r1 = up(ab0, 4), up(ab1, 4)
        return (
            jnp.where(lower_half, ab0, r0), jnp.where(lower_half, ab1, r1),
            jnp.where(lower_half, r0, ab0), jnp.where(lower_half, r1, ab1),
        )

    def step(g, carry):
        po, px, pz, p2o, p2x, heavy, held, lower, inverse, value = carry
        at = pl.multiple_of(g * ROWS, ROWS)
        o = [own[f, pl.ds(at, ROWS)] for f in range(FIELDS)]
        xz = [split(east_tile[f, pl.ds(at, ROWS)], west_tile[f, pl.ds(at, ROWS)]) for f in range(FIELDS)]
        x, z = [q[0] for q in xz], [q[1] for q in xz]
        pressures = []
        for block, total in ((o, po), (x, px), (z, pz)):
            inside, more = prefix(0.5 * density(block[0], block[1]))
            block.append(inside + total)
            pressures.append(total + more)
        level = tier_level + (LEVELS * g).astype(jnp.float32)
        around = [around_own(*q, shifted(rim[n], g)) for n, q in enumerate(zip(o, x))]
        weight = weights(level, depth_own, own_faces)
        o2 = update(weight, turn, o, *[[q[n] for q in around] for n in range(4)])
        around = [around_x(*q, shifted(rim_x[n], g)) for n, q in enumerate(zip(o, x, z))]
        x2 = update(
            weights(level, depth_x, x_faces), turn, x, *[[q[n] for q in around] for n in range(4)]
        )
        for block, total in ((o2, p2o), (x2, p2x)):
            inside, more = prefix(0.5 * density(block[0], block[1]))
            block.append(inside + total)
            pressures.append(total + more)
        around = [around_own(*q, shifted(rim_new[n], g)) for n, q in enumerate(zip(o2, x2))]
        done = update(weight, turn, o2, *[[q[n] for q in around] for n in range(4)])

        new_heavy = up(density(done[0], done[1]), COLUMNS)
        rise = density(done[0], done[1]) - jnp.where(tier == 0, heavy, new_heavy)
        a = ambient_all * (0.2 + 1.0 / (1.0 + 10.0 * jnp.maximum(rise, 0.0)))
        a = jnp.where(jnp.logical_and(weight[2], level > 0.5), a, 0.0)
        uppers = repeated(a)
        fields = per_level(done)
        xs = (held,) + fields[:3]
        lowers = (lower,) + uppers[:3]
        dets = []
        last, before = None, inverse
        for n in range(LEVELS):
            main = 1.0 + (lowers[n] + uppers[n])
            square = lowers[n] * lowers[n]
            if n == 0:
                det = main - square * before
            elif n == 1:
                det = main * last - square
            else:
                det = main * last - square * before
            dets.append(det)
            last, before = det, last
        for n in range(LEVELS):
            inverse = 1.0 / dets[n]
            if n > 0:
                inverse = inverse * dets[n - 1]
            value = (xs[n] + lowers[n] * value) * inverse
            y_out[LEVELS * g + n] = value
            r_out[LEVELS * g + n] = uppers[n] * inverse
        return (*pressures, new_heavy, fields[3], uppers[3], inverse, value)

    zero = jnp.zeros((ROWS, SPAN), jnp.float32)
    carry = (zero,) * 8 + (zero + 1.0, zero)
    for c, first in enumerate(starts):
        for copy in tiles[c]:
            copy.wait_recv()
        carry = lax.fori_loop(first, min(first + CHUNK, groups), step, carry, unroll=2)

    for part in tiles:
        for copy in part:
            copy.wait_send()
    for copy in statics:
        copy.wait_send()

    @pl.when(top)
    def _():
        to_a.wait_send()

    @pl.when(b_other)
    def _():
        to_b.wait_send()

    @pl.when(inner)
    def _():
        for copy in northward:
            copy.wait_send()

    @pl.when(above)
    def _():
        for copy in southward:
            copy.wait_send()


def substitute(levels, y, r, t_out, s_out, u_out, v_out, result, sem):
    outs = (t_out, s_out, u_out, v_out)
    cuts = [0, levels // 3, 2 * levels // 3, levels]
    current = y[levels]
    result[levels - 1] = current
    copies = []
    for n in range(len(cuts) - 2, -1, -1):
        lo, hi = cuts[n], cuts[n + 1]
        for k in range(min(hi, levels - 1) - 1, lo - 1, -1):
            current = y[k + 1] + r[k + 1] * current
            result[k] = current
        for f in range(FIELDS):
            copies.append(pltpu.make_async_copy(
                result.at[lo:hi, COLUMNS * f:COLUMNS * (f + 1), :], outs[f].at[lo:hi], sem.at[n, f]
            ))
            copies[-1].start()
    for copy in copies:
        copy.wait()


def solution(mesh):
    lon_count, lat_count = mesh.shape["lon"], mesh.shape["lat"]

    def shards(*args):
        levels = args[0].shape[0]
        groups = pl.cdiv(levels, LEVELS)
        chunks = pl.cdiv(groups, CHUNK)
        f32 = jnp.float32
        vmem = pl.BlockSpec(memory_space=pltpu.VMEM)
        anywhere = pl.BlockSpec(memory_space=pl.ANY)
        y, r = pl.pallas_call(
            functools.partial(halo_and_levels, levels, lon_count, lat_count),
            out_shape=[jax.ShapeDtypeStruct((groups * LEVELS, ROWS, SPAN), f32)] * 2,
            in_specs=[anywhere] * 7,
            out_specs=[vmem] * 2,
            scratch_shapes=[
                pltpu.VMEM((FIELDS, groups * ROWS, SPAN), f32),
                pltpu.VMEM((FIELDS, groups * ROWS, SPAN), f32),
                pltpu.VMEM((FIELDS, groups * ROWS, SPAN), f32),
                pltpu.VMEM((3, COLUMNS, SPAN), jnp.int32),
                pltpu.VMEM((3, COLUMNS, SPAN), f32),
                pltpu.VMEM((COLUMNS, SPAN), f32),
                pltpu.VMEM((FIELDS, ROWS, SPAN), f32),
                pltpu.VMEM((3, FIELDS, ROWS, SPAN), f32),
                pltpu.VMEM((3, FIELDS, ROWS, SPAN), f32),
                pltpu.VMEM((FIELDS + 1, ROWS, SPAN), f32),
                pltpu.VMEM((FIELDS + 1, ROWS, SPAN), f32),
                pltpu.VMEM((FIELDS + 1, ROWS, SPAN), f32),
                pltpu.SemaphoreType.DMA((8,)),
                pltpu.SemaphoreType.DMA((2, chunks, FIELDS)),
                pltpu.SemaphoreType.DMA((2, chunks, FIELDS)),
                pltpu.SemaphoreType.DMA((2, 2)),
                pltpu.SemaphoreType.DMA((2, 2)),
                pltpu.SemaphoreType.DMA((8,)),
                pltpu.SemaphoreType.DMA((6,)),
            ],
            compiler_params=pltpu.CompilerParams(collective_id=0, has_side_effects=True),
        )(*args)
        return pl.pallas_call(
            functools.partial(substitute, levels),
            out_shape=[jax.ShapeDtypeStruct(args[0].shape, f32)] * FIELDS,
            in_specs=[vmem] * 2,
            out_specs=[anywhere] * FIELDS,
            scratch_shapes=[
                pltpu.VMEM((levels, ROWS, SPAN), f32),
                pltpu.SemaphoreType.DMA((3, FIELDS)),
            ],
        )(y, r)

    wide, flat = P(None, "lon", "lat"), P("lon", "lat")
    return jax.shard_map(
        shards,
        mesh=mesh,
        in_specs=(wide,) * 4 + (flat,) * 3,
        out_specs=(wide,) * 4,
        check_vma=False,
    )
```

time: 127 us -> 34.9 us (0.27)
  the two profiles are of different devices: /device:TPU:56 before, /device:TPU:9 now
where the time goes in v1:
time: 34.9 us; the launch traced here: 34.7 us
  Pallas kernels  34.1 us (98%)
  between operations  0.64 us (2%)
    pallas_call x1, Pallas kernels, shards(): pl.pallas_call(functools.partial(halo_and_levels, levels, lon_count, lat_...  32.1 us
    pallas_call x1, Pallas kernels, shards(): pl.pallas_call(functools.partial(substitute, levels), out_shape=[jax.Shap...  1.96 us

profile of v1, /device:TPU:9, one launch (start us, length us, event | category | flops | bytes accessed | tf_op | source)
XLA Modules:
  0.0 34.7 jit_solution(712938606100698658)
XLA Ops:
  0.6 32.1 %shard_map.102 = (f32[76,8,128]{2,1,0:T(8,128)}, f32[76,8,128]{2,1,0:T(8,128)}) custom-call(f32[75,2,128]{2,1,0:T(2,128)} %t_in.1, f32[75,2,128]{2,1,0:T(2,128)} %s_in.1, f32[75,2,128]{2,1,0:T(2,128)} %u_in.1, f32[75,2,128]{2,1,0:T(2,128)} %v_in.1, s32[2,128]{1,0:T(2,128)} %flooded_in.1, f32[2,128]{1,0:T(2,128)} %lateral_in.1, f32[2,128]{1,0:T(2,128)} %ambient_in.1), custom_call_target="tpu_custom_call" | custom-call | tf_op jit(solution)/shard_map/pallas_call | solution.py:477
  32.8 2.0 %shard_map.103 = (f32[75,2,128]{2,1,0:T(2,128)}, f32[75,2,128]{2,1,0:T(2,128)}, f32[75,2,128]{2,1,0:T(2,128)}, f32[75,2,128]{2,1,0:T(2,128)}) custom-call(f32[76,8,128]{2,1,0:T(8,128)} %get-tuple-element.6.y, f32[76,8,128]{2,1,0:T(8,128)} %get-tuple-element.7.r), custom_call_target="tpu_custom_call" | custom-call | tf_op jit(solution)/shard_map/pallas_call | solution.py:505

commit v2 on v1

--- a/solution.py
+++ b/solution.py
@@ -14,7 +14,10 @@
 SPAN = 128
 LEVELS = 4
 ROWS = LEVELS * COLUMNS
-CHUNK = 4
+
+
+def cuts_of(groups):
+    return [0, *range(3, groups - 1, 4), groups]
 
 
 def density(t, s):
@@ -139,59 +142,83 @@
     northward = (edge(0, me, north, 0), edge(1, west, north, 1), edge(2, east, north, 2))
     southward = (edge(3, me, south, 3), edge(4, west, south, 4), edge(5, east, south, 5))
 
-    @pl.when(top)
-    def _():
-        to_a.start()
-
-    @pl.when(b_other)
-    def _():
-        to_b.start()
-
-    @pl.when(b_self)
-    def _():
-        b_copy.start()
-
-    @pl.when(inner)
-    def _():
-        for copy in northward:
-            copy.start()
-
-    @pl.when(above)
-    def _():
-        for copy in southward:
-            copy.start()
-
     sides = ((east, west_tile), (west, east_tile))
-    statics = []
-    for side, (lon, _) in enumerate(sides):
-        for n, (src, dst) in enumerate(((flooded_in, flooded), (lateral_in, lateral))):
-            statics.append(pltpu.make_async_remote_copy(
+    statics = [
+        [
+            pltpu.make_async_remote_copy(
                 src_ref=src, dst_ref=dst.at[1 + side],
                 send_sem=static_send.at[side, n], recv_sem=static_recv.at[side, n],
                 device_id=(lon, row), device_id_type=MESH,
-            ))
-    starts = list(range(0, groups, CHUNK))
+            )
+            for n, (src, dst) in enumerate(((flooded_in, flooded), (lateral_in, lateral)))
+        ]
+        for side, (lon, _) in enumerate(sides)
+    ]
+    cuts = cuts_of(groups)
     tiles = []
-    for c, first in enumerate(starts):
-        lo = first * ROWS
-        hi = min((first + CHUNK) * ROWS, levels * COLUMNS)
-        part = []
-        for f in range(FIELDS):
-            for side, (lon, dst) in enumerate(sides):
-                part.append(pltpu.make_async_remote_copy(
+    for c, (first, end) in enumerate(zip(cuts, cuts[1:])):
+        lo, hi = first * ROWS, min(end * ROWS, levels * COLUMNS)
+        tiles.append([
+            [
+                pltpu.make_async_remote_copy(
                     src_ref=flat[f].at[lo:hi], dst_ref=dst.at[f, lo:hi],
                     send_sem=ew_send.at[side, c, f], recv_sem=ew_recv.at[side, c, f],
                     device_id=(lon, row), device_id_type=MESH,
-                ))
-        tiles.append(part)
-    for copy in statics:
+                )
+                for f in range(FIELDS)
+            ]
+            for side, (lon, dst) in enumerate(sides)
+        ])
+
+    eastward, westward = 0, 1
+
+    def send_tiles(side, chunks):
+        for c in chunks:
+            for copy in tiles[c][side]:
+                copy.start()
+
+    @pl.when(top)
+    def _():
+        to_a.start()
+
+    @pl.when(b_other)
+    def _():
+        to_b.start()
+
+    @pl.when(b_self)
+    def _():
+        b_copy.start()
+
+    @pl.when(inner)
+    def _():
+        northward[2].start()
+
+    @pl.when(above)
+    def _():
+        southward[2].start()
+
+    for copy in statics[eastward]:
         copy.start()
-    for part in tiles:
-        for copy in part:
-            copy.start()
-
-    for copy in statics:
-        copy.wait_recv()
+    send_tiles(eastward, range(1))
+
+    @pl.when(inner)
+    def _():
+        northward[0].start()
+        northward[1].start()
+
+    @pl.when(above)
+    def _():
+        southward[0].start()
+        southward[1].start()
+
+    send_tiles(eastward, range(1, len(tiles)))
+    for copy in statics[westward]:
+        copy.start()
+    send_tiles(westward, range(len(tiles)))
+
+    for side in statics:
+        for copy in side:
+            copy.wait_recv()
 
     @pl.when(above)
     def _():
@@ -403,27 +430,34 @@
                 det = main * last - square * before
             dets.append(det)
             last, before = det, last
+        ys, rs = [], []
         for n in range(LEVELS):
             inverse = 1.0 / dets[n]
             if n > 0:
                 inverse = inverse * dets[n - 1]
             value = (xs[n] + lowers[n] * value) * inverse
-            y_out[LEVELS * g + n] = value
-            r_out[LEVELS * g + n] = uppers[n] * inverse
+            ys.append(value)
+            rs.append(uppers[n] * inverse)
+        y, r = ys[-1], rs[-1]
+        for n in range(LEVELS - 1, -1, -1):
+            if n < LEVELS - 1:
+                y, r = ys[n] + rs[n] * y, rs[n] * r
+            y_out[LEVELS * g + n] = y
+            r_out[LEVELS * g + n] = r
         return (*pressures, new_heavy, fields[3], uppers[3], inverse, value)
 
     zero = jnp.zeros((ROWS, SPAN), jnp.float32)
     carry = (zero,) * 8 + (zero + 1.0, zero)
-    for c, first in enumerate(starts):
-        for copy in tiles[c]:
-            copy.wait_recv()
-        carry = lax.fori_loop(first, min(first + CHUNK, groups), step, carry, unroll=2)
-
-    for part in tiles:
-        for copy in part:
-            copy.wait_send()
-    for copy in statics:
-        copy.wait_send()
+    for c, (first, end) in enumerate(zip(cuts, cuts[1:])):
+        for side in tiles[c]:
+            for copy in side:
+                copy.wait_recv()
+        carry = lax.fori_loop(first, end, step, carry, unroll=2)
+
+    for part in (*tiles, statics):
+        for side in part:
+            for copy in side:
+                copy.wait_send()
 
     @pl.when(top)
     def _():
@@ -446,18 +480,24 @@
 
 def substitute(levels, y, r, t_out, s_out, u_out, v_out, result, sem):
     outs = (t_out, s_out, u_out, v_out)
-    cuts = [0, levels // 3, 2 * levels // 3, levels]
-    current = y[levels]
-    result[levels - 1] = current
+    groups = pl.cdiv(levels, LEVELS)
+    cuts = [0, groups // 3, 2 * groups // 3, groups]
     copies = []
-    for n in range(len(cuts) - 2, -1, -1):
-        lo, hi = cuts[n], cuts[n + 1]
-        for k in range(min(hi, levels - 1) - 1, lo - 1, -1):
-            current = y[k + 1] + r[k + 1] * current
-            result[k] = current
+    below = jnp.zeros((ROWS, SPAN), jnp.float32)
+    for part in range(len(cuts) - 2, -1, -1):
+        for g in range(cuts[part + 1] - 1, cuts[part] - 1, -1):
+            at = LEVELS * g
+            rows = [y[at + n] + r[at + n] * below for n in range(LEVELS)]
+            below = rows[0]
+            for n in range(LEVELS):
+                if at + n > 0:
+                    result[at + n - 1] = rows[n]
+        lo = max(LEVELS * cuts[part] - 1, 0)
+        hi = LEVELS * cuts[part + 1] - 1
         for f in range(FIELDS):
             copies.append(pltpu.make_async_copy(
-                result.at[lo:hi, COLUMNS * f:COLUMNS * (f + 1), :], outs[f].at[lo:hi], sem.at[n, f]
+                result.at[lo:hi, COLUMNS * f:COLUMNS * (f + 1), :], outs[f].at[lo:hi],
+                sem.at[part, f],
             ))
             copies[-1].start()
     for copy in copies:
@@ -470,13 +510,13 @@
     def shards(*args):
         levels = args[0].shape[0]
         groups = pl.cdiv(levels, LEVELS)
-        chunks = pl.cdiv(groups, CHUNK)
+        chunks = len(cuts_of(groups)) - 1
         f32 = jnp.float32
         vmem = pl.BlockSpec(memory_space=pltpu.VMEM)
         anywhere = pl.BlockSpec(memory_space=pl.ANY)
         y, r = pl.pallas_call(
             functools.partial(halo_and_levels, levels, lon_count, lat_count),
-            out_shape=[jax.ShapeDtypeStruct((groups * LEVELS, ROWS, SPAN), f32)] * 2,
+            out_shape=[pltpu.VMEM((groups * LEVELS, ROWS, SPAN), f32)] * 2,
             in_specs=[anywhere] * 7,
             out_specs=[vmem] * 2,
             scratch_shapes=[
@@ -508,10 +548,10 @@
             in_specs=[vmem] * 2,
             out_specs=[anywhere] * FIELDS,
             scratch_shapes=[
-                pltpu.VMEM((levels, ROWS, SPAN), f32),
+                pltpu.VMEM((groups * LEVELS - 1, ROWS, SPAN), f32),
                 pltpu.SemaphoreType.DMA((3, FIELDS)),
             ],
-        )(y, r)
+        )(*(pltpu.with_memory_space_constraint(q, pltpu.VMEM) for q in (y, r)))
 
     wide, flat = P(None, "lon", "lat"), P("lon", "lat")
     return jax.shard_map(

time: 34.9 us -> 33 us (0.946)
  the two profiles are of different devices: /device:TPU:9 before, /device:TPU:8 now
where the time goes in v2:
time: 33 us; the launch traced here: 32.8 us
  Pallas kernels  32.2 us (98%)
  between operations  0.64 us (2%)
    pallas_call x1, Pallas kernels, shards(): pl.pallas_call(functools.partial(halo_and_levels, levels, lon_count, lat_...  31.4 us
    pallas_call x1, Pallas kernels, shards(): pl.pallas_call(functools.partial(substitute, levels), out_shape=[jax.Shap...  0.82 us

profile of v2, /device:TPU:8, one launch (start us, length us, event | category | flops | bytes accessed | tf_op | source)
XLA Modules:
  0.0 32.8 jit_solution(8366669969894676432)
XLA Ops:
  0.6 31.4 %shard_map.102 = (f32[76,8,128]{2,1,0:T(8,128)S(1)}, f32[76,8,128]{2,1,0:T(8,128)S(1)}) custom-call(f32[75,2,128]{2,1,0:T(2,128)} %t_in.1, f32[75,2,128]{2,1,0:T(2,128)} %s_in.1, f32[75,2,128]{2,1,0:T(2,128)} %u_in.1, f32[75,2,128]{2,1,0:T(2,128)} %v_in.1, s32[2,128]{1,0:T(2,128)} %flooded_in.1, f32[2,128]{1,0:T(2,128)} %lateral_in.1, f32[2,128]{1,0:T(2,128)} %ambient_in.1), custom_call_target="tpu_custom_call" | custom-call | tf_op jit(solution)/shard_map/pallas_call | solution.py:517
  32.0 0.8 %shard_map.103 = (f32[75,2,128]{2,1,0:T(2,128)}, f32[75,2,128]{2,1,0:T(2,128)}, f32[75,2,128]{2,1,0:T(2,128)}, f32[75,2,128]{2,1,0:T(2,128)}) custom-call(f32[76,8,128]{2,1,0:T(8,128)S(1)} %get-tuple-element.6.y, f32[76,8,128]{2,1,0:T(8,128)S(1)} %get-tuple-element.7.r), custom_call_target="tpu_custom_call" | custom-call | tf_op jit(solution)/shard_map/pallas_call | solution.py:545

commit v3 on v2

--- a/solution.py
+++ b/solution.py
@@ -12,6 +12,7 @@
 FIELDS = 4
 COLUMNS = 2
 SPAN = 128
+SEGMENT = 24
 LEVELS = 4
 ROWS = LEVELS * COLUMNS
 
@@ -159,14 +160,11 @@
     for c, (first, end) in enumerate(zip(cuts, cuts[1:])):
         lo, hi = first * ROWS, min(end * ROWS, levels * COLUMNS)
         tiles.append([
-            [
-                pltpu.make_async_remote_copy(
-                    src_ref=flat[f].at[lo:hi], dst_ref=dst.at[f, lo:hi],
-                    send_sem=ew_send.at[side, c, f], recv_sem=ew_recv.at[side, c, f],
-                    device_id=(lon, row), device_id_type=MESH,
-                )
-                for f in range(FIELDS)
-            ]
+            pltpu.make_async_remote_copy(
+                src_ref=own.at[:, lo:hi], dst_ref=dst.at[:, lo:hi],
+                send_sem=ew_send.at[side, c], recv_sem=ew_recv.at[side, c],
+                device_id=(lon, row), device_id_type=MESH,
+            )
             for side, (lon, dst) in enumerate(sides)
         ])
 
@@ -174,8 +172,7 @@
 
     def send_tiles(side, chunks):
         for c in chunks:
-            for copy in tiles[c][side]:
-                copy.start()
+            tiles[c][side].start()
 
     @pl.when(top)
     def _():
@@ -199,7 +196,11 @@
 
     for copy in statics[eastward]:
         copy.start()
-    send_tiles(eastward, range(1))
+    run_last = lax.rem(me, SEGMENT) == SEGMENT - 1
+
+    @pl.when(run_last)
+    def _():
+        send_tiles(eastward, range(len(tiles)))
 
     @pl.when(inner)
     def _():
@@ -211,7 +212,10 @@
         southward[0].start()
         southward[1].start()
 
-    send_tiles(eastward, range(1, len(tiles)))
+    @pl.when(jnp.logical_not(run_last))
+    def _():
+        send_tiles(eastward, range(len(tiles)))
+
     for copy in statics[westward]:
         copy.start()
     send_tiles(westward, range(len(tiles)))
@@ -449,15 +453,13 @@
     zero = jnp.zeros((ROWS, SPAN), jnp.float32)
     carry = (zero,) * 8 + (zero + 1.0, zero)
     for c, (first, end) in enumerate(zip(cuts, cuts[1:])):
-        for side in tiles[c]:
-            for copy in side:
-                copy.wait_recv()
+        for copy in tiles[c]:
+            copy.wait_recv()
         carry = lax.fori_loop(first, end, step, carry, unroll=2)
 
-    for part in (*tiles, statics):
-        for side in part:
-            for copy in side:
-                copy.wait_send()
+    for part in (*tiles, *statics):
+        for copy in part:
+            copy.wait_send()
 
     @pl.when(top)
     def _():
@@ -533,8 +535,8 @@
                 pltpu.VMEM((FIELDS + 1, ROWS, SPAN), f32),
                 pltpu.VMEM((FIELDS + 1, ROWS, SPAN), f32),
                 pltpu.SemaphoreType.DMA((8,)),
-                pltpu.SemaphoreType.DMA((2, chunks, FIELDS)),
-                pltpu.SemaphoreType.DMA((2, chunks, FIELDS)),
+                pltpu.SemaphoreType.DMA((2, chunks)),
+                pltpu.SemaphoreType.DMA((2, chunks)),
                 pltpu.SemaphoreType.DMA((2, 2)),
                 pltpu.SemaphoreType.DMA((2, 2)),
                 pltpu.SemaphoreType.DMA((8,)),

time: 33 us -> 32.4 us (0.982)
  Pallas kernels: 32.2 us -> 31.6 us
    pallas_call x1, Pallas kernels: 31.4 us -> 30.7 us  [shards(): pl.pallas_call(functools.partial(halo_and_levels, levels, lon_count, lat_...]
where the time goes in v3:
time: 32.4 us; the launch traced here: 32.2 us
  Pallas kernels  31.6 us (98%)
  between operations  0.64 us (2%)
    pallas_call x1, Pallas kernels, shards(): pl.pallas_call(functools.partial(halo_and_levels, levels, lon_count, lat_...  30.7 us
    pallas_call x1, Pallas kernels, shards(): pl.pallas_call(functools.partial(substitute, levels), out_shape=[jax.Shap...  0.82 us

profile of v3, /device:TPU:8, one launch (start us, length us, event | category | flops | bytes accessed | tf_op | source)
XLA Modules:
  0.0 32.2 jit_solution(16929591564009815343)
XLA Ops:
  0.6 30.7 %shard_map.102 = (f32[76,8,128]{2,1,0:T(8,128)S(1)}, f32[76,8,128]{2,1,0:T(8,128)S(1)}) custom-call(f32[75,2,128]{2,1,0:T(2,128)} %t_in.1, f32[75,2,128]{2,1,0:T(2,128)} %s_in.1, f32[75,2,128]{2,1,0:T(2,128)} %u_in.1, f32[75,2,128]{2,1,0:T(2,128)} %v_in.1, s32[2,128]{1,0:T(2,128)} %flooded_in.1, f32[2,128]{1,0:T(2,128)} %lateral_in.1, f32[2,128]{1,0:T(2,128)} %ambient_in.1), custom_call_target="tpu_custom_call" | custom-call | tf_op jit(solution)/shard_map/pallas_call | solution.py:519
  31.4 0.8 %shard_map.103 = (f32[75,2,128]{2,1,0:T(2,128)}, f32[75,2,128]{2,1,0:T(2,128)}, f32[75,2,128]{2,1,0:T(2,128)}, f32[75,2,128]{2,1,0:T(2,128)}) custom-call(f32[76,8,128]{2,1,0:T(8,128)S(1)} %get-tuple-element.6.y, f32[76,8,128]{2,1,0:T(8,128)S(1)} %get-tuple-element.7.r), custom_call_target="tpu_custom_call" | custom-call | tf_op jit(solution)/shard_map/pallas_call | solution.py:547

commit v4 on v3

--- a/solution.py
+++ b/solution.py
@@ -62,8 +62,20 @@
     def greet(lon, lat):
         pl.semaphore_signal(barrier, inc=1, device_id=(lon, lat), device_id_type=MESH)
 
+    @pl.when(inner)
+    def _():
+        greet(me, north)
+        greet(west, north)
+        greet(east, north)
+
+    @pl.when(above)
+    def _():
+        greet(me, south)
+        greet(west, south)
+        greet(east, south)
+
+    greet(west, row)
     greet(east, row)
-    greet(west, row)
 
     @pl.when(top)
     def _():
@@ -72,18 +84,6 @@
     @pl.when(b_other)
     def _():
         greet(fold_b, row)
-
-    @pl.when(inner)
-    def _():
-        greet(me, north)
-        greet(east, north)
-        greet(west, north)
-
-    @pl.when(above)
-    def _():
-        greet(me, south)
-        greet(east, south)
-        greet(west, south)
 
     flat = [x.reshape(levels * COLUMNS, SPAN) for x in fields_in]
     local = [
@@ -256,7 +256,7 @@
         return s + jnp.where(tier >= 2, up(s, 2 * COLUMNS), 0.0), pair + up(pair, 2 * COLUMNS)
 
     def packed_pressure(t, s):
-        inside, total = prefix(0.5 * density(t, s))
+        inside, total = prefix((0.25 * DT) * density(t, s))
         for n in (4, 8, 16, 32, 64):
             total = total + jnp.where(lane >= n, along(total, n), 0.0)
         return inside + jnp.where(lane >= 4, along(total, 4), 0.0)
@@ -302,9 +302,9 @@
         for f in range(FIELDS):
             x = (keep * cells[f] + ce * e[f]) + (cw * w[f] + (cn * n[f] + cs * s[f]))
             if f == 2:
-                x = x + (turn * cells[3] - (0.5 * DT) * (e[4] - w[4]))
+                x = x + (turn * cells[3] - (e[4] - w[4]))
             if f == 3:
-                x = x - (turn * cells[2] + (0.5 * DT) * (n[4] - s[4]))
+                x = x - (turn * cells[2] + (n[4] - s[4]))
             out.append(jnp.where(wet, x, 0.0))
         return out
 
@@ -395,7 +395,7 @@
         x, z = [q[0] for q in xz], [q[1] for q in xz]
         pressures = []
         for block, total in ((o, po), (x, px), (z, pz)):
-            inside, more = prefix(0.5 * density(block[0], block[1]))
+            inside, more = prefix((0.25 * DT) * density(block[0], block[1]))
             block.append(inside + total)
             pressures.append(total + more)
         level = tier_level + (LEVELS * g).astype(jnp.float32)
@@ -407,14 +407,15 @@
             weights(level, depth_x, x_faces), turn, x, *[[q[n] for q in around] for n in range(4)]
         )
         for block, total in ((o2, p2o), (x2, p2x)):
-            inside, more = prefix(0.5 * density(block[0], block[1]))
+            inside, more = prefix((0.25 * DT) * density(block[0], block[1]))
             block.append(inside + total)
             pressures.append(total + more)
         around = [around_own(*q, shifted(rim_new[n], g)) for n, q in enumerate(zip(o2, x2))]
         done = update(weight, turn, o2, *[[q[n] for q in around] for n in range(4)])
 
-        new_heavy = up(density(done[0], done[1]), COLUMNS)
-        rise = density(done[0], done[1]) - jnp.where(tier == 0, heavy, new_heavy)
+        weighed = density(done[0], done[1])
+        new_heavy = up(weighed, COLUMNS)
+        rise = weighed - jnp.where(tier == 0, heavy, new_heavy)
         a = ambient_all * (0.2 + 1.0 / (1.0 + 10.0 * jnp.maximum(rise, 0.0)))
         a = jnp.where(jnp.logical_and(weight[2], level > 0.5), a, 0.0)
         uppers = repeated(a)

time: 32.4 us -> 32.4 us (level)
  no operation moved by 1% of the time
where the time goes in v4:
time: 32.4 us; the launch traced here: 32.2 us
  Pallas kernels  31.6 us (98%)
  between operations  0.64 us (2%)
    pallas_call x1, Pallas kernels, shards(): pl.pallas_call(functools.partial(halo_and_levels, levels, lon_count, lat_...  30.8 us
    pallas_call x1, Pallas kernels, shards(): pl.pallas_call(functools.partial(substitute, levels), out_shape=[jax.Shap...  0.82 us

profile of v4, /device:TPU:8, one launch (start us, length us, event | category | flops | bytes accessed | tf_op | source)
XLA Modules:
  0.0 32.2 jit_solution(12291467717931363325)
XLA Ops:
  0.6 30.8 %shard_map.102 = (f32[76,8,128]{2,1,0:T(8,128)S(1)}, f32[76,8,128]{2,1,0:T(8,128)S(1)}) custom-call(f32[75,2,128]{2,1,0:T(2,128)} %t_in.1, f32[75,2,128]{2,1,0:T(2,128)} %s_in.1, f32[75,2,128]{2,1,0:T(2,128)} %u_in.1, f32[75,2,128]{2,1,0:T(2,128)} %v_in.1, s32[2,128]{1,0:T(2,128)} %flooded_in.1, f32[2,128]{1,0:T(2,128)} %lateral_in.1, f32[2,128]{1,0:T(2,128)} %ambient_in.1), custom_call_target="tpu_custom_call" | custom-call | tf_op jit(solution)/shard_map/pallas_call | solution.py:520
  31.4 0.8 %shard_map.103 = (f32[75,2,128]{2,1,0:T(2,128)}, f32[75,2,128]{2,1,0:T(2,128)}, f32[75,2,128]{2,1,0:T(2,128)}, f32[75,2,128]{2,1,0:T(2,128)}) custom-call(f32[76,8,128]{2,1,0:T(8,128)S(1)} %get-tuple-element.6.y, f32[76,8,128]{2,1,0:T(8,128)S(1)} %get-tuple-element.7.r), custom_call_target="tpu_custom_call" | custom-call | tf_op jit(solution)/shard_map/pallas_call | solution.py:548

commit v5 on v4

--- a/solution.py
+++ b/solution.py
@@ -220,35 +220,6 @@
         copy.start()
     send_tiles(westward, range(len(tiles)))
 
-    for side in statics:
-        for copy in side:
-            copy.wait_recv()
-
-    @pl.when(above)
-    def _():
-        for copy in northward:
-            copy.wait_recv()
-
-    @pl.when(inner)
-    def _():
-        for copy in southward:
-            copy.wait_recv()
-
-    @pl.when(top)
-    def _():
-        to_a.wait_recv()
-
-    @pl.when(b_other)
-    def _():
-        to_b.wait_recv()
-
-    @pl.when(b_self)
-    def _():
-        b_copy.wait()
-
-    def sideways(o, x):
-        return jnp.where(even, up(o, -1), up(x, 1)), jnp.where(even, up(x, -1), up(o, 1))
-
     def prefix(d):
         two = up(d, COLUMNS)
         s = d + jnp.where(tier >= 1, two, 0.0)
@@ -266,6 +237,39 @@
         for n in (4, 8, 16, 32, 64):
             x = x + along(x, n)
         return x
+
+    own_edge = [pack[f] for f in range(FIELDS)]
+    o_depth, o_mix = every_quad(own_edge[0], groups), (0.5 * DT) * every_quad(own_edge[0], groups + 1)
+    own_edge.append(packed_pressure(own_edge[0], own_edge[1]))
+
+    for side in statics:
+        for copy in side:
+            copy.wait_recv()
+
+    @pl.when(above)
+    def _():
+        for copy in northward:
+            copy.wait_recv()
+
+    @pl.when(inner)
+    def _():
+        for copy in southward:
+            copy.wait_recv()
+
+    @pl.when(top)
+    def _():
+        to_a.wait_recv()
+
+    @pl.when(b_other)
+    def _():
+        to_b.wait_recv()
+
+    @pl.when(b_self)
+    def _():
+        b_copy.wait()
+
+    def sideways(o, x):
+        return jnp.where(even, up(o, -1), up(x, 1)), jnp.where(even, up(x, -1), up(o, 1))
 
     for f in range(FIELDS):
         sign = 1.0 if f < 2 else -1.0
@@ -308,13 +312,11 @@
             out.append(jnp.where(wet, x, 0.0))
         return out
 
-    own_edge = [pack[f] for f in range(FIELDS)]
     cells = [rim[f] for f in range(FIELDS)]
     cells_x = [rim_x[f] for f in range(FIELDS)]
     rim_depth, rim_mix = every_quad(cells[0], groups), (0.5 * DT) * every_quad(cells[0], groups + 1)
     x_depth, x_mix = every_quad(cells_x[0], groups), (0.5 * DT) * every_quad(cells_x[0], groups + 1)
-    o_depth, o_mix = every_quad(own_edge[0], groups), (0.5 * DT) * every_quad(own_edge[0], groups + 1)
-    for block in (own_edge, cells, cells_x):
+    for block in (cells, cells_x):
         block.append(packed_pressure(block[0], block[1]))
     rim[4] = cells[4]
     rim_x[4] = cells_x[4]

time: 32.4 us -> 32.4 us (level)
  no operation moved by 1% of the time
where the time goes in v5:
time: 32.4 us; the launch traced here: 32.2 us
  Pallas kernels  31.6 us (98%)
  between operations  0.64 us (2%)
    pallas_call x1, Pallas kernels, shards(): pl.pallas_call(functools.partial(halo_and_levels, levels, lon_count, lat_...  30.8 us
    pallas_call x1, Pallas kernels, shards(): pl.pallas_call(functools.partial(substitute, levels), out_shape=[jax.Shap...  0.82 us

profile of v5, /device:TPU:8, one launch (start us, length us, event | category | flops | bytes accessed | tf_op | source)
XLA Modules:
  0.0 32.2 jit_solution(16705654064756619557)
XLA Ops:
  0.6 30.8 %shard_map.102 = (f32[76,8,128]{2,1,0:T(8,128)S(1)}, f32[76,8,128]{2,1,0:T(8,128)S(1)}) custom-call(f32[75,2,128]{2,1,0:T(2,128)} %t_in.1, f32[75,2,128]{2,1,0:T(2,128)} %s_in.1, f32[75,2,128]{2,1,0:T(2,128)} %u_in.1, f32[75,2,128]{2,1,0:T(2,128)} %v_in.1, s32[2,128]{1,0:T(2,128)} %flooded_in.1, f32[2,128]{1,0:T(2,128)} %lateral_in.1, f32[2,128]{1,0:T(2,128)} %ambient_in.1), custom_call_target="tpu_custom_call" | custom-call | tf_op jit(solution)/shard_map/pallas_call | solution.py:522
  31.4 0.8 %shard_map.103 = (f32[75,2,128]{2,1,0:T(2,128)}, f32[75,2,128]{2,1,0:T(2,128)}, f32[75,2,128]{2,1,0:T(2,128)}, f32[75,2,128]{2,1,0:T(2,128)}) custom-call(f32[76,8,128]{2,1,0:T(8,128)S(1)} %get-tuple-element.6.y, f32[76,8,128]{2,1,0:T(8,128)S(1)} %get-tuple-element.7.r), custom_call_target="tpu_custom_call" | custom-call | tf_op jit(solution)/shard_map/pallas_call | solution.py:550

commit v6 on v5

--- a/solution.py
+++ b/solution.py
@@ -18,7 +18,7 @@
 
 
 def cuts_of(groups):
-    return [0, *range(3, groups - 1, 4), groups]
+    return [0, *range(5, groups - 1, 6), groups]
 
 
 def density(t, s):

time: 32.4 us -> 32.5 us (level)
  no operation moved by 1% of the time
where the time goes in v6:
time: 32.5 us; the launch traced here: 32.3 us
  Pallas kernels  31.7 us (98%)
  between operations  0.64 us (2%)
    pallas_call x1, Pallas kernels, shards(): pl.pallas_call(functools.partial(halo_and_levels, levels, lon_count, lat_...  30.9 us
    pallas_call x1, Pallas kernels, shards(): pl.pallas_call(functools.partial(substitute, levels), out_shape=[jax.Shap...  0.82 us

profile of v6, /device:TPU:8, one launch (start us, length us, event | category | flops | bytes accessed | tf_op | source)
XLA Modules:
  0.0 32.3 jit_solution(6088481680773868358)
XLA Ops:
  0.6 30.9 %shard_map.102 = (f32[76,8,128]{2,1,0:T(8,128)S(1)}, f32[76,8,128]{2,1,0:T(8,128)S(1)}) custom-call(f32[75,2,128]{2,1,0:T(2,128)} %t_in.1, f32[75,2,128]{2,1,0:T(2,128)} %s_in.1, f32[75,2,128]{2,1,0:T(2,128)} %u_in.1, f32[75,2,128]{2,1,0:T(2,128)} %v_in.1, s32[2,128]{1,0:T(2,128)} %flooded_in.1, f32[2,128]{1,0:T(2,128)} %lateral_in.1, f32[2,128]{1,0:T(2,128)} %ambient_in.1), custom_call_target="tpu_custom_call" | custom-call | tf_op jit(solution)/shard_map/pallas_call | solution.py:522
  31.5 0.8 %shard_map.103 = (f32[75,2,128]{2,1,0:T(2,128)}, f32[75,2,128]{2,1,0:T(2,128)}, f32[75,2,128]{2,1,0:T(2,128)}, f32[75,2,128]{2,1,0:T(2,128)}) custom-call(f32[76,8,128]{2,1,0:T(8,128)S(1)} %get-tuple-element.6.y, f32[76,8,128]{2,1,0:T(8,128)S(1)} %get-tuple-element.7.r), custom_call_target="tpu_custom_call" | custom-call | tf_op jit(solution)/shard_map/pallas_call | solution.py:550
